TPU v7x, 32 devices: a whole 2x2x4 slice. The times are simulated.
32 devices in a mesh: section: 4 (over x, core), expert: 8 (over z, y).
Axes of the slice: x: 2, y: 2, z: 4, core: 2. Of those that a mesh axis runs over, the one named last changes fastest.
Arguments:
- tokens: bfloat16 [2048, 7168], P('expert', 'section'), may hold values from -6 to 6
- gate_up: bfloat16 [8, 7168, 2, 1024], P('expert', 'section'), may hold values from -0.0625 to 0.0625
- down_weight: bfloat16 [8, 1024, 7168], P('expert', None, 'section'), may hold values from -0.1875 to 0.1875
- expert_ids: int32 [2048, 8], P('expert'), may hold values from 0 to 31, all different within a row; in each aligned block of 256 rows (0 to 255, 256 to 511, ...) at most 96 rows name the same one
- gate_values: float32 [2048, 8], P('expert'), may hold values from 0.2 to 1
- owner_map: int32 [8], replicated, may hold values from 0 to 7, each once
Outputs:
- mixed: bfloat16 [2048, 7168], P('expert', 'section')
Inputs may be any that keep to these rules, and one draw needn't show every extreme that they name: `expert_ids`: each row names 8 different experts; among the 256 rows of one index of expert no expert is named more than 96 times. `owner_map`: each owner holds exactly one expert.
All inputs are finite; a program needn't handle non-finite values.
Results may differ from a plain program's by a relative error of at most 0.028.
Values may be sent and summed in bfloat16 or wider, within the bound.
A program may use at most 64 MiB of HBM per device.

v0:
```python
import jax
import jax.numpy as jnp
from jax import lax
from jax.sharding import PartitionSpec as P

TOP = 8


def on_device(tokens, gate_up, down_weight, expert_ids, gate_values, owner_map):
    tok_rows = tokens.shape[0]
    experts = lax.axis_size("expert")
    slot_count = max(2, 3 * tok_rows * TOP // (8 * experts))
    device_ids = jnp.arange(experts, dtype=jnp.int32)
    named = (expert_ids[:, :, None] == device_ids[None, None, :]).astype(jnp.float32)
    placed = (owner_map[:, None] == device_ids[None, :]).astype(jnp.float32)
    routed = jnp.einsum("tjk,kd->tjd", named, placed)
    picked = jnp.sum(routed, axis=1)
    weighted = jnp.einsum("tj,tjd->td", gate_values, routed, precision=lax.Precision.HIGHEST)
    ranks = jnp.cumsum(picked, axis=0) - 1.0
    slot_hot = picked[:, :, None] * (
        ranks[:, :, None] == jnp.arange(slot_count, dtype=jnp.float32)[None, None, :]
    )
    slot_mask = slot_hot.astype(jnp.bfloat16)
    sending = jnp.einsum(
        "tdc,tf->dcf", slot_mask, tokens, preferred_element_type=jnp.float32
    ).astype(jnp.bfloat16)
    weight_in = gate_up[0]
    weight_out = down_weight[0]
    partial_sums = jnp.einsum(
        "scd,dgf->scgf",
        lax.all_to_all(sending, "expert", split_axis=0, concat_axis=0, tiled=True),
        weight_in,
        preferred_element_type=jnp.float32,
    )
    shares = lax.psum_scatter(
        partial_sums.astype(jnp.bfloat16), "section", scatter_dimension=0, tiled=True
    ).astype(jnp.float32)
    active = (jax.nn.silu(shares[:, :, 0]) * shares[:, :, 1]).astype(jnp.bfloat16)
    hidden = lax.all_gather(active, "section", axis=0, tiled=True)
    expert_out = jnp.einsum(
        "scf,fd->scd", hidden, weight_out, preferred_element_type=jnp.float32
    ).astype(jnp.bfloat16)
    arrived = lax.all_to_all(expert_out, "expert", split_axis=0, concat_axis=0, tiled=True)
    slot_weight = jnp.einsum("tdc,td->dc", slot_hot, weighted, precision=lax.Precision.HIGHEST)
    scaled = slot_weight[:, :, None] * arrived.astype(jnp.float32)
    upper_part = lax.optimization_barrier(scaled.astype(jnp.bfloat16))
    lower_part = (scaled - upper_part.astype(jnp.float32)).astype(jnp.bfloat16)
    mixed = jnp.einsum("tdc,dcf->tf", slot_mask, upper_part, preferred_element_type=jnp.float32)
    mixed = mixed + jnp.einsum(
        "tdc,dcf->tf", slot_mask, lower_part, preferred_element_type=jnp.float32
    )
    return mixed.astype(jnp.bfloat16)


def solution(mesh):
    placed = (
        P("expert", "section"),
        P("expert", "section", None, None),
        P("expert", None, "section"),
        P("expert", None),
        P("expert", None),
        P(),
    )
    return jax.shard_map(
        on_device, mesh=mesh, in_specs=placed, out_specs=P("expert", "section"), check_vma=False
    )
```

profile of v0, /device:TPU:0, one launch (start us, length us, event | category | flops | bytes accessed | tf_op | source)
XLA Modules:
  0.0 234.9 jit_solution(4801547036297499093)
XLA Ops:
  6.5 0.0 copy-start
  6.5 0.0 reduce-scatter.2.cloned.1.call-start
  6.5 0.9 multiply_reduce_fusion
  7.5 0.6 reduce-window.6
  8.1 0.2 slice_reduce_fusion
  8.3 0.1 add_bitcast_fusion
  8.4 0.0 copy-done
  8.4 0.0 copy-start.1
  8.4 0.9 convolution_convert_fusion
  9.3 70.0 %all_to_all.10 = bf16[8,96,1792]{2,1,0:T(8,128)(2,1)S(1)} all-to-all(bf16[8,96,1792]{2,1,0:T(8,128)(2,1)S(1)} %convolution_convert_fusion), channel_id=1, replica_groups=mesh['section'=4,'expert'=8] {'expert'}, dimensions={0} | all-to-all | bytes 5505024 | tf_op jit(solution)/shard_map/all_to_all | solution.py:31
  79.2 0.0 copy-done.1
  79.2 7.4 %fusion.15 = bf16[8,96,2,1024]{3,1,2,0:T(8,128)(2,1)} fusion(bf16[1792,2,1024]{2,1,0:T(2,128)(2,1)S(1)} %bitcast.62, bf16[8,96,1792]{2,1,0:T(8,128)(2,1)S(1)} %all_to_all.10), kind=kOutput, calls=%fused_computation.17 | convolution fusion | flops 5638717440 | bytes 13238272 | tf_op jit(solution)/shard_map/scd,dgf->scgf/dot_general | solution.py:29
  86.7 0.0 reduce-scatter.2.cloned.1.call-update
  86.7 0.0 all-gather.2.cloned.1.call-start
  86.8 36.7 %reduce-scatter.2.cloned.1.call-done = bf16[2,96,2,1024]{3,1,2,0:T(8,128)(2,1)} async-done(((bf16[8,96,2,1024]{3,1,2,0:T(8,128)(2,1)}), bf16[2,96,2,1024]{3,1,2,0:T(8,128)(2,1)}) %reduce-scatter.2.cloned.1.call-update) | async-done | bytes 786448 | tf_op jit(solution)/shard_map/reduce_scatter | solution.py:35
  123.4 1.3 convert_element_type.39
  124.7 1.0 fusion.24
  125.7 0.0 all-gather.2.cloned.1.call-update
  125.7 19.8 %all-gather.2.cloned.1.call-done = bf16[8,96,1024]{2,1,0:T(8,128)(2,1)} async-done(((bf16[2,96,1024]{2,1,0:T(8,128)(2,1)}), bf16[8,96,1024]{2,1,0:T(8,128)(2,1)}) %all-gather.2.cloned.1.call-update) | async-done | bytes 1572880 | tf_op jit(solution)/shard_map/all_gather | solution.py:39
  145.5 7.1 %fusion.6 = bf16[8,96,1792]{2,1,0:T(8,128)(2,1)} fusion(bf16[8,96,1024]{2,1,0:T(8,128)(2,1)} %all-gather.2.cloned.1.call-done, bf16[1,1024,1792]{2,1,0:T(8,128)(2,1)} %param.8), kind=kOutput, calls=%fused_computation.8 | convolution fusion | flops 2819948544 | bytes 7995392 | tf_op jit(solution)/shard_map/scf,fd->scd/dot_general | solution.py:40
  152.6 5.5 %all-to-all-start.1 = ((bf16[8,96,1792]{2,1,0:T(8,128)(2,1)}), bf16[8,96,1792]{2,1,0:T(8,128)(2,1)}, u32[]{:S(2)}, u32[]{:S(2)}) async-start(bf16[8,96,1792]{2,1,0:T(8,128)(2,1)} %fusion.6), calls=%async_computation.2 | async-start | bytes 5505024 | tf_op jit(solution)/shard_map/all_to_all | solution.py:43
  158.1 0.8 fusion.20
  158.9 62.0 %all-to-all-done.1 = bf16[8,96,1792]{2,1,0:T(8,128)(2,1)} async-done(((bf16[8,96,1792]{2,1,0:T(8,128)(2,1)}), bf16[8,96,1792]{2,1,0:T(8,128)(2,1)}, u32[]{:S(2)}, u32[]{:S(2)}) %all-to-all-start.1) | async-done | bytes 2752544 | tf_op jit(solution)/shard_map/all_to_all | solution.py:43
  220.9 2.3 fusion.3
  223.2 0.9 convolution_bitcast_fusion
  224.1 3.9 %fusion.14 = bf16[256,1792]{1,0:T(8,128)(2,1)} fusion(f32[256,1792]{1,0:T(8,128)S(1)} %convolution_bitcast_fusion, bf16[8,96,1792]{2,1,0:T(8,128)(2,1)S(1)} %fusion.3, bf16[8,96,1792]{2,1,0:T(8,128)(2,1)} %all-to-all-done.1, f32[8,96]{1,0:T(8,128)S(1)} %bitcast.61, f32[256,8]{0,1:T(8,128)S(1)} %get-tuple-element.6, f32[256,8]{0,1:T(8,128)S(1)} %add_bitcast_fusion), kind=kOutput, calls=%fused_computation.16 | convolution fusion | flops 712835072 | bytes 8276992 | tf_op jit(solution)/shard_map/tdc,dcf->tf/dot_general | solution.py:49
  (2 shorter events, 0.0 us)
Async XLA Ops:
  6.5 1.8 copy-start
  6.5 116.9 %reduce-scatter.2.cloned.1.call-start = ((), (), s32[]{:S(2)}) async-start(), calls=%async_computation.3 | async-start | bytes 3932160 | tf_op jit(solution)/shard_map/reduce_scatter | solution.py:35
  8.4 70.9 %copy-start.1 = (bf16[1,1792,2,1024]{3,2,1,0:T(2,128)(2,1)S(1)}, bf16[1,1792,2,1024]{3,2,1,0:T(2,128)(2,1)}, u32[]{:S(2)}) copy-start(bf16[1,1792,2,1024]{3,2,1,0:T(2,128)(2,1)} %param.7) | copy-start | bytes 22020100
  86.7 58.8 %all-gather.2.cloned.1.call-start = ((), (), s32[]{:S(2)}) async-start(), calls=%async_computation.4 | async-start | bytes 1966080 | tf_op jit(solution)/shard_map/all_gather | solution.py:39
  152.6 68.3 %all-to-all-start.1 = ((bf16[8,96,1792]{2,1,0:T(8,128)(2,1)}), bf16[8,96,1792]{2,1,0:T(8,128)(2,1)}, u32[]{:S(2)}, u32[]{:S(2)}) async-start(bf16[8,96,1792]{2,1,0:T(8,128)(2,1)} %fusion.6), calls=%async_computation.2 | async-start | bytes 5505024 | tf_op jit(solution)/shard_map/all_to_all | solution.py:43
Sparse Core Ops, SparseCore 0:
  86.8 36.5 reduce-scatter.1
  125.9 19.6 all-gather.1
where the time goes:
time: 235 us
  waiting for transfers between devices  118 us (50%)
  blocking collectives  70 us (30%)
  matrix products  22 us (9%)
  between operations  13.4 us (6%)
  starting transfers between devices  5.56 us (2%)
  other arithmetic  5.26 us (2%)
    all_to_all x1, blocking collectives, on_device(): lax.all_to_all(sending, 'expert', split_axis=0, concat_axis=0, tiled=True)  70 us
    all_to_all x1, waiting for transfers between devices, on_device(): lax.all_to_all(expert_out, 'expert', split_axis=0, concat_axis=0, tiled=T...  62 us
    reduce_scatter x1, waiting for transfers between devices, on_device(): lax.psum_scatter(partial_sums.astype(jnp.bfloat16), 'section', scatter_di...  36.7 us
    all_gather x1, waiting for transfers between devices, on_device(): hidden = lax.all_gather(active, 'section', axis=0, tiled=True)  19.8 us
    dot_general x1, matrix products, on_device(): jnp.einsum('scd,dgf->scgf', lax.all_to_all(sending, 'expert', split_axis=...  7.45 us
    dot_general x1, matrix products, on_device(): jnp.einsum('scf,fd->scd', hidden, weight_out, preferred_element_type=jnp....  7.08 us
    all_to_all x1, starting transfers between devices, on_device(): lax.all_to_all(expert_out, 'expert', split_axis=0, concat_axis=0, tiled=T...  5.52 us
  transfers between devices with their start and end apart: 3, of which 3 were waited for; matrix products, arithmetic and copies ran while one was open for 0% of the time, Pallas kernels for 0%

commit v1 on v0

--- a/solution.py
+++ b/solution.py
@@ -1,15 +1,192 @@
+import functools
+
 import jax
 import jax.numpy as jnp
 from jax import lax
+from jax.experimental import pallas as pl
+from jax.experimental.pallas import tpu as pltpu
 from jax.sharding import PartitionSpec as P
 
-TOP = 8
-
-
-def on_device(tokens, gate_up, down_weight, expert_ids, gate_values, owner_map):
+MESH = pl.DeviceIdType.MESH
+F32, BF16 = jnp.float32, jnp.bfloat16
+
+
+def partner(me, k, n):
+    out, bit = me, 1
+    while bit < n:
+        out = out + ((k // bit) % 2) * (1 - 2 * ((me // bit) % 2)) * bit
+        bit *= 2
+    return out
+
+
+def layer_kernel(
+    n, q,
+    tok, code, wts, win_hbm, wout_hbm, out,
+    win, wout, send, recv, psend, precv, hid, osend, back, acc,
+    wsem, asend, arecv, bsend, brecv, csend, crecv, dsend, drecv,
+):
+    me = lax.axis_index("expert")
+    sec = lax.axis_index("section")
+    slots, width = send.shape[1], send.shape[2]
+    rows = tok.shape[0]
+    cols = hid.shape[3]
+
+    load_in = pltpu.make_async_copy(win_hbm, win, wsem.at[0])
+    load_out = pltpu.make_async_copy(wout_hbm, wout, wsem.at[1])
+    load_in.start()
+    load_out.start()
+
+    barrier = pltpu.get_barrier_semaphore()
+
+    def greet(k, c):
+        pl.semaphore_signal(barrier, inc=1, device_id={"expert": partner(me, k, n)}, device_id_type=MESH)
+        return c
+
+    lax.fori_loop(1, n, greet, 0)
+    for r in range(1, q):
+        pl.semaphore_signal(barrier, inc=1, device_id={"section": (sec + r) % q}, device_id_type=MESH)
+    pl.semaphore_wait(barrier, n + q - 2)
+
+    slot_iota = lax.broadcasted_iota(jnp.int32, (slots, rows), 0)
+
+    def a_copy(k):
+        return pltpu.make_async_remote_copy(
+            src_ref=send.at[k], dst_ref=recv.at[k], send_sem=asend.at[k], recv_sem=arecv.at[k],
+            device_id={"expert": partner(me, k, n)}, device_id_type=MESH)
+
+    def d_copy(k):
+        return pltpu.make_async_remote_copy(
+            src_ref=osend.at[k], dst_ref=back.at[k], send_sem=dsend.at[k], recv_sem=drecv.at[k],
+            device_id={"expert": partner(me, k, n)}, device_id_type=MESH)
+
+    def pick(k):
+        hot = (code[partner(me, k, n)] == slot_iota).astype(F32).astype(BF16)
+        return jnp.dot(hot, tok[...], preferred_element_type=F32).astype(BF16)
+
+    def dispatch(i, c):
+        k = n - i
+        send[k] = pick(k)
+        a_copy(k).start()
+        return c
+
+    lax.fori_loop(1, n, dispatch, 0)
+    recv[0] = pick(0)
+    load_in.wait()
+    load_out.wait()
+
+    def project(k):
+        @pl.when(k != 0)
+        def _():
+            a_copy(k).wait_recv()
+
+        for step in range(q):
+            r = (step + 1) % q
+            j = (sec + r) % q
+            at = pl.ds(pl.multiple_of(j * cols, cols), cols)
+            for g in range(2):
+                part = jnp.dot(recv[k], win[g, :, at], preferred_element_type=F32)
+                psend[k, r, :, g * cols:(g + 1) * cols] = part.astype(BF16)
+            if r:
+                pltpu.make_async_remote_copy(
+                    src_ref=psend.at[k, r], dst_ref=precv.at[k, r - 1],
+                    send_sem=bsend.at[k], recv_sem=brecv.at[k],
+                    device_id={"section": j}, device_id_type=MESH).start()
+
+    def b_all(k):
+        return pltpu.make_async_remote_copy(
+            src_ref=psend.at[k, pl.ds(1, q - 1)], dst_ref=precv.at[k],
+            send_sem=bsend.at[k], recv_sem=brecv.at[k],
+            device_id={"section": (sec + 1) % q}, device_id_type=MESH)
+
+    def activate(k):
+        b_all(k).wait_recv()
+        total = psend[k, 0].astype(F32)
+        for r in range(q - 1):
+            total = total + precv[k, r].astype(F32)
+        gate, up = total[:, :cols], total[:, cols:]
+        hid[k, sec] = (gate / (1.0 + jnp.exp(-gate)) * up).astype(BF16)
+        for r in range(1, q):
+            pltpu.make_async_remote_copy(
+                src_ref=hid.at[k, sec], dst_ref=hid.at[k, sec],
+                send_sem=csend.at[k], recv_sem=crecv.at[k],
+                device_id={"section": (sec + r) % q}, device_id_type=MESH).start()
+
+    def c_all(k):
+        return pltpu.make_async_remote_copy(
+            src_ref=hid.at[k, pl.ds(0, q - 1)], dst_ref=hid.at[k, pl.ds(0, q - 1)],
+            send_sem=csend.at[k], recv_sem=crecv.at[k],
+            device_id={"section": (sec + 1) % q}, device_id_type=MESH)
+
+    def finish(k):
+        c_all(k).wait_recv()
+        res = jnp.dot(hid[k, 0], wout[:cols, :], preferred_element_type=F32)
+        for j in range(1, q):
+            res = res + jnp.dot(hid[k, j], wout[j * cols:(j + 1) * cols, :], preferred_element_type=F32)
+
+        @pl.when(k == 0)
+        def _():
+            back[0] = res.astype(BF16)
+
+        @pl.when(k != 0)
+        def _():
+            osend[k] = res.astype(BF16)
+            d_copy(k).start()
+
+    def stage(i, c):
+        @pl.when(i < n)
+        def _():
+            project((n - i) % n)
+
+        @pl.when((i >= 1) & (i <= n))
+        def _():
+            activate((n - i + 1) % n)
+
+        @pl.when(i >= 2)
+        def _():
+            finish((n - i + 2) % n)
+
+        return c
+
+    lax.fori_loop(0, n + 2, stage, 0)
+
+    acc[...] = jnp.zeros_like(acc)
+
+    def combine(i, c):
+        k = (n - i) % n
+        d = partner(me, k, n)
+
+        @pl.when(k != 0)
+        def _():
+            d_copy(k).wait_recv()
+
+        w = jnp.where(code[d] == slot_iota, wts[d], 0.0)
+        upper = w.astype(BF16)
+        lower = (w - upper.astype(F32)).astype(BF16)
+        dims = (((0,), (0,)), ((), ()))
+        acc[...] += lax.dot_general(upper, back[k], dims, preferred_element_type=F32) + lax.dot_general(
+            lower, back[k], dims, preferred_element_type=F32)
+        return c
+
+    lax.fori_loop(0, n, combine, 0)
+    out[...] = acc[...].astype(out.dtype)
+
+    def drain(k, c):
+        @pl.when(k != 0)
+        def _():
+            a_copy(k).wait_send()
+            d_copy(k).wait_send()
+
+        b_all(k).wait_send()
+        c_all(k).wait_send()
+        return c
+
+    lax.fori_loop(0, n, drain, 0)
+
+
+def exchanged(tokens, gate_up, down_weight, expert_ids, gate_values, owner_map):
     tok_rows = tokens.shape[0]
     experts = lax.axis_size("expert")
-    slot_count = max(2, 3 * tok_rows * TOP // (8 * experts))
+    slot_count = max(2, 3 * tok_rows * expert_ids.shape[1] // (8 * experts))
     device_ids = jnp.arange(experts, dtype=jnp.int32)
     named = (expert_ids[:, :, None] == device_ids[None, None, :]).astype(jnp.float32)
     placed = (owner_map[:, None] == device_ids[None, :]).astype(jnp.float32)
@@ -52,6 +229,56 @@
     return mixed.astype(jnp.bfloat16)
 
 
+def on_device(tokens, gate_up, down_weight, expert_ids, gate_values, owner_map):
+    rows, width = tokens.shape
+    top = expert_ids.shape[1]
+    n, q = lax.axis_size("expert"), lax.axis_size("section")
+    slots = max(2, 3 * rows * top // (8 * n))
+    slots = -(-slots // 16) * 16
+    hidden = down_weight.shape[1]
+    cols = hidden // q
+    if width % 128 or cols % 128 or n & (n - 1):
+        return exchanged(tokens, gate_up, down_weight, expert_ids, gate_values, owner_map)
+
+    owners = jnp.arange(n, dtype=jnp.int32)
+    held = jnp.sum(jnp.where(owner_map[:, None] == owners[None, :], owners[:, None], 0), axis=0)
+    hits = expert_ids.T[None, :, :] == held[:, None, None]
+    picked = jnp.any(hits, axis=1)
+    weights = jnp.sum(jnp.where(hits, gate_values.T[None, :, :], 0.0), axis=1)
+    upto = (jnp.arange(rows)[:, None] <= jnp.arange(rows)[None, :]).astype(BF16)
+    ranks = jnp.dot(picked.astype(BF16), upto, preferred_element_type=F32).astype(jnp.int32) - 1
+    code = jnp.where(picked, ranks, -1)[:, None, :]
+    weights = weights[:, None, :]
+    weight_in = jnp.swapaxes(gate_up[0], 0, 1)
+
+    vmem = pl.BlockSpec(memory_space=pltpu.VMEM)
+    hbm = pl.BlockSpec(memory_space=pl.ANY)
+    dma = pltpu.SemaphoreType.DMA
+    return pl.pallas_call(
+        functools.partial(layer_kernel, n, q),
+        out_shape=jax.ShapeDtypeStruct((rows, width), BF16),
+        in_specs=[vmem, vmem, vmem, hbm, hbm],
+        out_specs=vmem,
+        scratch_shapes=[
+            pltpu.VMEM((2, width, hidden), BF16),
+            pltpu.VMEM((hidden, width), BF16),
+            pltpu.VMEM((n, slots, width), BF16),
+            pltpu.VMEM((n, slots, width), BF16),
+            pltpu.VMEM((n, q, slots, 2 * cols), BF16),
+            pltpu.VMEM((n, q - 1, slots, 2 * cols), BF16),
+            pltpu.VMEM((n, q, slots, cols), BF16),
+            pltpu.VMEM((n, slots, width), BF16),
+            pltpu.VMEM((n, slots, width), BF16),
+            pltpu.VMEM((rows, width), F32),
+            dma((2,)),
+            dma((n,)), dma((n,)), dma((n,)), dma((n,)), dma((n,)), dma((n,)), dma((n,)), dma((n,)),
+        ],
+        compiler_params=pltpu.CompilerParams(
+            collective_id=0, has_side_effects=True, vmem_limit_bytes=60 * 1024 * 1024
+        ),
+    )(tokens, code, weights, weight_in, down_weight[0])
+
+
 def solution(mesh):
     placed = (
         P("expert", "section"),

time: 235 us -> 150 us (0.64)
  Pallas kernels: 0 us -> 135 us
  waiting for transfers between devices: 118 us -> 0 us
  blocking collectives: 70 us -> 0 us
  matrix products: 22 us -> 0.15 us
  between operations: 13.4 us -> 0.02 us
  local copies, waits for them, and re-layouts: 0.17 us -> 11.8 us
  starting transfers between devices: 5.56 us -> 0 us
  other arithmetic: 5.26 us -> 2.33 us
    pallas_call x0 -> x1, Pallas kernels: none -> 135 us  [on_device(): pl.pallas_call(functools.partial(layer_kernel, n, q), out_shape=jax.Shape...]
    all_to_all x1 -> x0, blocking collectives: 70 us -> none  [on_device(): lax.all_to_all(sending, 'expert', split_axis=0, concat_axis=0, tiled=True)]
    all_to_all x1 -> x0, waiting for transfers between devices: 62 us -> none  [on_device(): lax.all_to_all(expert_out, 'expert', split_axis=0, concat_axis=0, tiled=T...]
    reduce_scatter x1 -> x0, waiting for transfers between devices: 36.7 us -> none  [on_device(): lax.psum_scatter(partial_sums.astype(jnp.bfloat16), 'section', scatter_di...]
    dot_general x7 -> x1, matrix products: 22 us -> 0.15 us  [on_device(): jnp.dot(picked.astype(BF16), upto, preferred_element_type=F32)]
    all_gather x1 -> x0, waiting for transfers between devices: 19.8 us -> none  [on_device(): hidden = lax.all_gather(active, 'section', axis=0, tiled=True)]
    unnamed x4 -> x2, local copies, waits for them, and re-layouts: 0.01 us -> 10.6 us
    all_to_all x1 -> x0, starting transfers between devices: 5.52 us -> none  [on_device(): lax.all_to_all(expert_out, 'expert', split_axis=0, concat_axis=0, tiled=T...]
  transfers between devices with their start and end apart: 3 -> 0, of which waited for: 3 -> 0; matrix products, arithmetic and copies ran while one was open for 0% -> 0% of each run, Pallas kernels for 0% -> 0%
where the time goes in v1:
time: 150 us; the launch traced here: 149 us
  Pallas kernels  135 us (90%)
  local copies, waits for them, and re-layouts  11.8 us (8%)
  other arithmetic  2.33 us (2%)
    pallas_call x1, Pallas kernels, on_device(): pl.pallas_call(functools.partial(layer_kernel, n, q), out_shape=jax.Shape...  135 us
    unnamed x2, local copies, waits for them, and re-layouts  10.6 us

profile of v1, /device:TPU:0, one launch (start us, length us, event | category | flops | bytes accessed | tf_op | source)
XLA Modules:
  0.0 149.4 jit_solution(10131440299767226388)
XLA Ops:
  0.0 0.7 select_reduce_fusion
  0.7 0.8 compare_reduce_fusion
  1.5 0.2 fusion.1
  1.7 0.6 broadcast_in_dim.42.code
  2.3 0.8 fusion.2
  3.1 0.6 broadcast_in_dim.45.wts
  3.7 8.4 %copy.10 = bf16[1,1792,2,1024]{3,1,2,0:T(8,128)(2,1)} copy(bf16[1,1792,2,1024]{3,2,1,0:T(2,128)(2,1)} %param.7) | data formatting | bytes 14680064 | tf_op args[1]
  12.1 135.1 %shard_map.64 = bf16[256,1792]{1,0:T(8,128)(2,1)} custom-call(bf16[256,1792]{1,0:T(8,128)(2,1)} %tok.1, s32[8,1,256]{2,1,0:T(1,128)} %broadcast_in_dim.42.code, f32[8,1,256]{2,1,0:T(1,128)} %broadcast_in_dim.45.wts, bf16[2,1792,1024]{2,1,0:T(8,128)(2,1)} %bitcast.9, bf16[1024,1792]{1,0:T(8,128)(2,1)} %bitcast.10), custom_call_target="tpu_custom_call" | custom-call | tf_op jit(solution)/shard_map/pallas_call | solution.py:257
  147.2 2.2 %copy.12 = bf16[256,1792]{1,0:T(8,128)(2,1)} copy(bf16[256,1792]{1,0:T(8,128)(2,1)} %shard_map.64) | data formatting | bytes 1835008

commit v2 on v1

--- a/solution.py
+++ b/solution.py
@@ -21,8 +21,8 @@
 
 def layer_kernel(
     n, q,
-    tok, code, wts, win_hbm, wout_hbm, out,
-    win, wout, send, recv, psend, precv, hid, osend, back, acc,
+    tok, ids, gates, owner, win_hbm, wout_hbm, out,
+    raw, win, wout, send, recv, psend, precv, hid, osend, back, acc, code, wts,
     wsem, asend, arecv, bsend, brecv, csend, crecv, dsend, drecv,
 ):
     me = lax.axis_index("expert")
@@ -31,7 +31,7 @@
     rows = tok.shape[0]
     cols = hid.shape[3]
 
-    load_in = pltpu.make_async_copy(win_hbm, win, wsem.at[0])
+    load_in = pltpu.make_async_copy(win_hbm, raw, wsem.at[0])
     load_out = pltpu.make_async_copy(wout_hbm, wout, wsem.at[1])
     load_in.start()
     load_out.start()
@@ -45,6 +45,21 @@
     lax.fori_loop(1, n, greet, 0)
     for r in range(1, q):
         pl.semaphore_signal(barrier, inc=1, device_id={"section": (sec + r) % q}, device_id_type=MESH)
+
+    def find(d, c):
+        held = jnp.int32(0)
+        for k in range(n):
+            held = held + jnp.where(owner[k] == d, k, 0)
+        hit = ids[...] == held
+        code[pl.ds(d, 1), :] = jnp.max(jnp.where(hit, 1, 0), axis=0, keepdims=True)
+        wts[pl.ds(d, 1), :] = jnp.sum(jnp.where(hit, gates[...], 0.0), axis=0, keepdims=True)
+        return c
+
+    lax.fori_loop(0, n, find, 0)
+    upto = lax.broadcasted_iota(jnp.int32, (rows, rows), 0) <= lax.broadcasted_iota(jnp.int32, (rows, rows), 1)
+    ranks = jnp.dot(
+        code[...].astype(F32).astype(BF16), jnp.where(upto, 1.0, 0.0).astype(BF16), preferred_element_type=F32)
+    code[...] = jnp.where(code[...] > 0, ranks.astype(jnp.int32) - 1, -1)
     pl.semaphore_wait(barrier, n + q - 2)
 
     slot_iota = lax.broadcasted_iota(jnp.int32, (slots, rows), 0)
@@ -60,7 +75,7 @@
             device_id={"expert": partner(me, k, n)}, device_id_type=MESH)
 
     def pick(k):
-        hot = (code[partner(me, k, n)] == slot_iota).astype(F32).astype(BF16)
+        hot = (code[pl.ds(partner(me, k, n), 1), :] == slot_iota).astype(F32).astype(BF16)
         return jnp.dot(hot, tok[...], preferred_element_type=F32).astype(BF16)
 
     def dispatch(i, c):
@@ -72,6 +87,14 @@
     lax.fori_loop(1, n, dispatch, 0)
     recv[0] = pick(0)
     load_in.wait()
+
+    def split(i, c):
+        part = pl.ds(pl.multiple_of(i * 128, 128), 128)
+        win[0, part, :] = raw[part, 0, :]
+        win[1, part, :] = raw[part, 1, :]
+        return c
+
+    lax.fori_loop(0, width // 128, split, 0)
     load_out.wait()
 
     def project(k):
@@ -159,7 +182,7 @@
         def _():
             d_copy(k).wait_recv()
 
-        w = jnp.where(code[d] == slot_iota, wts[d], 0.0)
+        w = jnp.where(code[pl.ds(d, 1), :] == slot_iota, wts[pl.ds(d, 1), :], 0.0)
         upper = w.astype(BF16)
         lower = (w - upper.astype(F32)).astype(BF16)
         dims = (((0,), (0,)), ((), ()))
@@ -240,16 +263,7 @@
     if width % 128 or cols % 128 or n & (n - 1):
         return exchanged(tokens, gate_up, down_weight, expert_ids, gate_values, owner_map)
 
-    owners = jnp.arange(n, dtype=jnp.int32)
-    held = jnp.sum(jnp.where(owner_map[:, None] == owners[None, :], owners[:, None], 0), axis=0)
-    hits = expert_ids.T[None, :, :] == held[:, None, None]
-    picked = jnp.any(hits, axis=1)
-    weights = jnp.sum(jnp.where(hits, gate_values.T[None, :, :], 0.0), axis=1)
-    upto = (jnp.arange(rows)[:, None] <= jnp.arange(rows)[None, :]).astype(BF16)
-    ranks = jnp.dot(picked.astype(BF16), upto, preferred_element_type=F32).astype(jnp.int32) - 1
-    code = jnp.where(picked, ranks, -1)[:, None, :]
-    weights = weights[:, None, :]
-    weight_in = jnp.swapaxes(gate_up[0], 0, 1)
+    weight_in = gate_up[0]
 
     vmem = pl.BlockSpec(memory_space=pltpu.VMEM)
     hbm = pl.BlockSpec(memory_space=pl.ANY)
@@ -257,9 +271,10 @@
     return pl.pallas_call(
         functools.partial(layer_kernel, n, q),
         out_shape=jax.ShapeDtypeStruct((rows, width), BF16),
-        in_specs=[vmem, vmem, vmem, hbm, hbm],
+        in_specs=[vmem, vmem, vmem, pl.BlockSpec(memory_space=pltpu.SMEM), hbm, hbm],
         out_specs=vmem,
         scratch_shapes=[
+            pltpu.VMEM((width, 2, hidden), BF16),
             pltpu.VMEM((2, width, hidden), BF16),
             pltpu.VMEM((hidden, width), BF16),
             pltpu.VMEM((n, slots, width), BF16),
@@ -270,13 +285,15 @@
             pltpu.VMEM((n, slots, width), BF16),
             pltpu.VMEM((n, slots, width), BF16),
             pltpu.VMEM((rows, width), F32),
+            pltpu.VMEM((n, rows), jnp.int32),
+            pltpu.VMEM((n, rows), F32),
             dma((2,)),
             dma((n,)), dma((n,)), dma((n,)), dma((n,)), dma((n,)), dma((n,)), dma((n,)), dma((n,)),
         ],
         compiler_params=pltpu.CompilerParams(
             collective_id=0, has_side_effects=True, vmem_limit_bytes=60 * 1024 * 1024
         ),
-    )(tokens, code, weights, weight_in, down_weight[0])
+    )(tokens, expert_ids.T, gate_values.T, owner_map, weight_in, down_weight[0])
 
 
 def solution(mesh):

time: 150 us -> 138 us (0.920)
  local copies, waits for them, and re-layouts: 11.8 us -> 2.16 us
  other arithmetic: 2.33 us -> 0 us
    unnamed x2 -> x1, local copies, waits for them, and re-layouts: 10.6 us -> 2.16 us
    reduce_sum x2 -> x0, other arithmetic: 1.54 us -> none  [the longest x1 0.8 us: on_device(): weights = jnp.sum(jnp.where(hits, gate_values.T[None, :, :], 0.0), axis=1)]
where the time goes in v2:
time: 138 us; the launch traced here: 137 us
  Pallas kernels  135 us (98%)
  local copies, waits for them, and re-layouts  2.16 us (2%)
    pallas_call x1, Pallas kernels, on_device(): pl.pallas_call(functools.partial(layer_kernel, n, q), out_shape=jax.Shape...  135 us

profile of v2, /device:TPU:0, one launch (start us, length us, event | category | flops | bytes accessed | tf_op | source)
XLA Modules:
  0.0 137.1 jit_solution(1569923975388117746)
XLA Ops:
  0.0 134.9 %shard_map.64 = bf16[256,1792]{1,0:T(8,128)(2,1)} custom-call(bf16[256,1792]{1,0:T(8,128)(2,1)} %tok.1, s32[8,256]{1,0:T(8,128)} %bitcast.6, f32[8,256]{1,0:T(8,128)} %bitcast.7, s32[8]{0:T(128)} %owner.1, bf16[1792,2,1024]{2,1,0:T(2,128)(2,1)} %bitcast.4, bf16[1024,1792]{1,0:T(8,128)(2,1)} %bitcast.5), custom_call_target="tpu_custom_call" | custom-call | tf_op jit(solution)/shard_map/pallas_call | solution.py:271
  134.9 2.2 %copy.8 = bf16[256,1792]{1,0:T(8,128)(2,1)} copy(bf16[256,1792]{1,0:T(8,128)(2,1)} %shard_map.64) | data formatting | bytes 1835008

commit v3 on v2

--- a/solution.py
+++ b/solution.py
@@ -22,14 +22,16 @@
 def layer_kernel(
     n, q,
     tok, ids, gates, owner, win_hbm, wout_hbm, out,
-    raw, win, wout, send, recv, psend, precv, hid, osend, back, acc, code, wts,
-    wsem, asend, arecv, bsend, brecv, csend, crecv, dsend, drecv,
+    raw, win, wout, send, recv, far, psend, precv, hid, osend, back, sums, met, acc, code, wts, table, mixer,
+    wsem, tsend, trecv, fsend, frecv, asend, arecv, bsend, brecv, csend, crecv, dsend, drecv, gsend, grecv,
 ):
     me = lax.axis_index("expert")
     sec = lax.axis_index("section")
-    slots, width = send.shape[1], send.shape[2]
-    rows = tok.shape[0]
+    half = n // 2
+    slots = send.shape[1]
+    rows, width = tok.shape
     cols = hid.shape[3]
+    pieces, piece = far.shape[0], far.shape[2]
 
     load_in = pltpu.make_async_copy(win_hbm, raw, wsem.at[0])
     load_out = pltpu.make_async_copy(wout_hbm, wout, wsem.at[1])
@@ -42,7 +44,7 @@
         pl.semaphore_signal(barrier, inc=1, device_id={"expert": partner(me, k, n)}, device_id_type=MESH)
         return c
 
-    lax.fori_loop(1, n, greet, 0)
+    lax.fori_loop(1, half + 1, greet, 0)
     for r in range(1, q):
         pl.semaphore_signal(barrier, inc=1, device_id={"section": (sec + r) % q}, device_id_type=MESH)
 
@@ -51,41 +53,74 @@
         for k in range(n):
             held = held + jnp.where(owner[k] == d, k, 0)
         hit = ids[...] == held
-        code[pl.ds(d, 1), :] = jnp.max(jnp.where(hit, 1, 0), axis=0, keepdims=True)
-        wts[pl.ds(d, 1), :] = jnp.sum(jnp.where(hit, gates[...], 0.0), axis=0, keepdims=True)
+        code[0, pl.ds(d, 1), :] = jnp.max(jnp.where(hit, 1, 0), axis=0, keepdims=True)
+        wts[0, pl.ds(d, 1), :] = jnp.sum(jnp.where(hit, gates[...], 0.0), axis=0, keepdims=True)
         return c
 
     lax.fori_loop(0, n, find, 0)
     upto = lax.broadcasted_iota(jnp.int32, (rows, rows), 0) <= lax.broadcasted_iota(jnp.int32, (rows, rows), 1)
     ranks = jnp.dot(
-        code[...].astype(F32).astype(BF16), jnp.where(upto, 1.0, 0.0).astype(BF16), preferred_element_type=F32)
-    code[...] = jnp.where(code[...] > 0, ranks.astype(jnp.int32) - 1, -1)
-    pl.semaphore_wait(barrier, n + q - 2)
+        code[0].astype(F32).astype(BF16), jnp.where(upto, 1.0, 0.0).astype(BF16), preferred_element_type=F32)
+    code[0] = jnp.where(code[0] > 0, ranks.astype(jnp.int32) - 1, -1)
+    pl.semaphore_wait(barrier, half + q - 1)
 
     slot_iota = lax.broadcasted_iota(jnp.int32, (slots, rows), 0)
+    across = {"expert": partner(me, half, n)}
+
+    def span(p):
+        return pl.ds(pl.multiple_of(p * piece, piece), piece)
+
+    def t_copy(ref, i):
+        return pltpu.make_async_remote_copy(
+            src_ref=ref.at[0], dst_ref=ref.at[1], send_sem=tsend.at[i], recv_sem=trecv.at[i],
+            device_id=across, device_id_type=MESH)
+
+    def f_copy(p):
+        return pltpu.make_async_remote_copy(
+            src_ref=tok.at[:, span(p)], dst_ref=far.at[p], send_sem=fsend.at[p], recv_sem=frecv.at[p],
+            device_id=across, device_id_type=MESH)
 
     def a_copy(k):
         return pltpu.make_async_remote_copy(
             src_ref=send.at[k], dst_ref=recv.at[k], send_sem=asend.at[k], recv_sem=arecv.at[k],
-            device_id={"expert": partner(me, k, n)}, device_id_type=MESH)
+            device_id={"expert": partner(me, k % half, n)}, device_id_type=MESH)
+
+    def a_part(k, p):
+        return pltpu.make_async_remote_copy(
+            src_ref=send.at[k, :, span(p)], dst_ref=recv.at[k, :, span(p)],
+            send_sem=asend.at[k], recv_sem=arecv.at[k],
+            device_id={"expert": partner(me, k % half, n)}, device_id_type=MESH)
 
     def d_copy(k):
         return pltpu.make_async_remote_copy(
             src_ref=osend.at[k], dst_ref=back.at[k], send_sem=dsend.at[k], recv_sem=drecv.at[k],
-            device_id={"expert": partner(me, k, n)}, device_id_type=MESH)
-
-    def pick(k):
-        hot = (code[pl.ds(partner(me, k, n), 1), :] == slot_iota).astype(F32).astype(BF16)
-        return jnp.dot(hot, tok[...], preferred_element_type=F32).astype(BF16)
+            device_id={"expert": partner(me, k % half, n)}, device_id_type=MESH)
+
+    def g_copy(p):
+        return pltpu.make_async_remote_copy(
+            src_ref=sums.at[p], dst_ref=met.at[p], send_sem=gsend.at[p], recv_sem=grecv.at[p],
+            device_id=across, device_id_type=MESH)
+
+    t_copy(code, 0).start()
+    t_copy(wts, 1).start()
+
+    def hot(side, k):
+        return (code[side, pl.ds(partner(me, k, n), 1), :] == slot_iota).astype(F32).astype(BF16)
 
     def dispatch(i, c):
-        k = n - i
-        send[k] = pick(k)
+        k = half - i
+        send[k] = jnp.dot(hot(0, k), tok[...], preferred_element_type=F32).astype(BF16)
         a_copy(k).start()
         return c
 
-    lax.fori_loop(1, n, dispatch, 0)
-    recv[0] = pick(0)
+    lax.fori_loop(1, half, dispatch, 0)
+
+    def cross(p, c):
+        f_copy(p).start()
+        return c
+
+    lax.fori_loop(0, pieces, cross, 0)
+    recv[0] = jnp.dot(hot(0, 0), tok[...], preferred_element_type=F32).astype(BF16)
     load_in.wait()
 
     def split(i, c):
@@ -96,9 +131,39 @@
 
     lax.fori_loop(0, width // 128, split, 0)
     load_out.wait()
+    t_copy(code, 0).wait_recv()
+    t_copy(wts, 1).wait_recv()
+
+    def weigh(side):
+        def one(k, c):
+            at = pl.ds(partner(me, k, n), 1)
+            table[pl.ds(pl.multiple_of(k * slots, 16), slots), :] = jnp.where(
+                code[side, at, :] == slot_iota, wts[side, at, :], 0.0)
+            return c
+
+        lax.fori_loop(0, half, one, 0)
+        turned = table[...].T
+        upper = turned.astype(BF16)
+        mixer[side, 0] = upper
+        mixer[side, 1] = (turned - upper.astype(F32)).astype(BF16)
+
+    weigh(0)
+    weigh(1)
+
+    def relay(p):
+        f_copy(p).wait_recv()
+        block = far[p]
+        recv[half, :, span(p)] = jnp.dot(hot(1, 0), block, preferred_element_type=F32).astype(BF16)
+
+        def one(k, c):
+            send[half + k, :, span(p)] = jnp.dot(hot(1, k), block, preferred_element_type=F32).astype(BF16)
+            a_part(half + k, p).start()
+            return c
+
+        lax.fori_loop(1, half, one, 0)
 
     def project(k):
-        @pl.when(k != 0)
+        @pl.when(k % half != 0)
         def _():
             a_copy(k).wait_recv()
 
@@ -146,55 +211,86 @@
         for j in range(1, q):
             res = res + jnp.dot(hid[k, j], wout[j * cols:(j + 1) * cols, :], preferred_element_type=F32)
 
-        @pl.when(k == 0)
-        def _():
-            back[0] = res.astype(BF16)
-
-        @pl.when(k != 0)
+        @pl.when(k % half == 0)
+        def _():
+            back[k] = res.astype(BF16)
+
+        @pl.when(k % half != 0)
         def _():
             osend[k] = res.astype(BF16)
             d_copy(k).start()
 
-    def stage(i, c):
+    def early(i, c):
+        project(i)
+
+        def some(p, e):
+            relay(p)
+            return e
+
+        lax.fori_loop(i * pieces // half, (i + 1) * pieces // half, some, 0)
+
+        @pl.when(i >= 1)
+        def _():
+            activate(i - 1)
+
+        @pl.when(i >= 2)
+        def _():
+            finish(i - 2)
+
+        return c
+
+    def late(i, c):
         @pl.when(i < n)
         def _():
-            project((n - i) % n)
-
-        @pl.when((i >= 1) & (i <= n))
-        def _():
-            activate((n - i + 1) % n)
-
-        @pl.when(i >= 2)
-        def _():
-            finish((n - i + 2) % n)
-
-        return c
-
-    lax.fori_loop(0, n + 2, stage, 0)
-
-    acc[...] = jnp.zeros_like(acc)
-
-    def combine(i, c):
-        k = (n - i) % n
-        d = partner(me, k, n)
-
-        @pl.when(k != 0)
-        def _():
-            d_copy(k).wait_recv()
-
-        w = jnp.where(code[pl.ds(d, 1), :] == slot_iota, wts[pl.ds(d, 1), :], 0.0)
-        upper = w.astype(BF16)
-        lower = (w - upper.astype(F32)).astype(BF16)
-        dims = (((0,), (0,)), ((), ()))
-        acc[...] += lax.dot_general(upper, back[k], dims, preferred_element_type=F32) + lax.dot_general(
-            lower, back[k], dims, preferred_element_type=F32)
-        return c
-
-    lax.fori_loop(0, n, combine, 0)
-    out[...] = acc[...].astype(out.dtype)
+            project(i)
+
+        @pl.when(i <= n)
+        def _():
+            activate(i - 1)
+
+        finish(i - 2)
+        return c
+
+    lax.fori_loop(0, half, early, 0)
+    lax.fori_loop(half, n + 2, late, 0)
+
+    def arrived(first):
+        def one(k, c):
+            d_copy(first + k).wait_recv()
+            return c
+
+        lax.fori_loop(1, half, one, 0)
+
+    def mixed(side, p):
+        rhs = back[pl.ds(side * half, half), :, span(p)].reshape(half * slots, piece)
+        return jnp.dot(mixer[side, 0], rhs, preferred_element_type=F32) + jnp.dot(
+            mixer[side, 1], rhs, preferred_element_type=F32)
+
+    arrived(half)
+
+    def give(p, c):
+        sums[p] = mixed(1, p).astype(BF16)
+        g_copy(p).start()
+        return c
+
+    lax.fori_loop(0, pieces, give, 0)
+    arrived(0)
+
+    def own(p, c):
+        acc[p] = mixed(0, p)
+        return c
+
+    lax.fori_loop(0, pieces, own, 0)
+
+    def close(p, c):
+        g_copy(p).wait_recv()
+        out[:, span(p)] = (acc[p] + met[p].astype(F32)).astype(out.dtype)
+        return c
+
+    lax.fori_loop(0, pieces, close, 0)
 
     def drain(k, c):
-        @pl.when(k != 0)
+        @pl.when(k % half != 0)
         def _():
             a_copy(k).wait_send()
             d_copy(k).wait_send()
@@ -204,6 +300,15 @@
         return c
 
     lax.fori_loop(0, n, drain, 0)
+
+    def drain_pieces(p, c):
+        f_copy(p).wait_send()
+        g_copy(p).wait_send()
+        return c
+
+    lax.fori_loop(0, pieces, drain_pieces, 0)
+    t_copy(code, 0).wait_send()
+    t_copy(wts, 1).wait_send()
 
 
 def exchanged(tokens, gate_up, down_weight, expert_ids, gate_values, owner_map):
@@ -260,10 +365,13 @@
     slots = -(-slots // 16) * 16
     hidden = down_weight.shape[1]
     cols = hidden // q
-    if width % 128 or cols % 128 or n & (n - 1):
+    if width % 128 or cols % 128 or n < 4 or n & (n - 1):
         return exchanged(tokens, gate_up, down_weight, expert_ids, gate_values, owner_map)
 
     weight_in = gate_up[0]
+    half = n // 2
+    piece = 256 if width % 256 == 0 else 128
+    pieces = width // piece
 
     vmem = pl.BlockSpec(memory_space=pltpu.VMEM)
     hbm = pl.BlockSpec(memory_space=pl.ANY)
@@ -279,16 +387,22 @@
             pltpu.VMEM((hidden, width), BF16),
             pltpu.VMEM((n, slots, width), BF16),
             pltpu.VMEM((n, slots, width), BF16),
+            pltpu.VMEM((pieces, rows, piece), BF16),
             pltpu.VMEM((n, q, slots, 2 * cols), BF16),
             pltpu.VMEM((n, q - 1, slots, 2 * cols), BF16),
             pltpu.VMEM((n, q, slots, cols), BF16),
             pltpu.VMEM((n, slots, width), BF16),
             pltpu.VMEM((n, slots, width), BF16),
-            pltpu.VMEM((rows, width), F32),
-            pltpu.VMEM((n, rows), jnp.int32),
-            pltpu.VMEM((n, rows), F32),
-            dma((2,)),
+            pltpu.VMEM((pieces, rows, piece), BF16),
+            pltpu.VMEM((pieces, rows, piece), BF16),
+            pltpu.VMEM((pieces, rows, piece), F32),
+            pltpu.VMEM((2, n, rows), jnp.int32),
+            pltpu.VMEM((2, n, rows), F32),
+            pltpu.VMEM((half * slots, rows), F32),
+            pltpu.VMEM((2, 2, rows, half * slots), BF16),
+            dma((2,)), dma((2,)), dma((2,)), dma((pieces,)), dma((pieces,)),
             dma((n,)), dma((n,)), dma((n,)), dma((n,)), dma((n,)), dma((n,)), dma((n,)), dma((n,)),
+            dma((pieces,)), dma((pieces,)),
         ],
         compiler_params=pltpu.CompilerParams(
             collective_id=0, has_side_effects=True, vmem_limit_bytes=60 * 1024 * 1024

time: 138 us -> 140 us (1.014)
  Pallas kernels: 135 us -> 138 us
    pallas_call x1, Pallas kernels: 135 us -> 138 us  [on_device(): pl.pallas_call(functools.partial(layer_kernel, n, q), out_shape=jax.Shape...]
where the time goes in v3:
time: 140 us
  Pallas kernels  138 us (99%)
  local copies, waits for them, and re-layouts  2.16 us (2%)
    pallas_call x1, Pallas kernels, on_device(): pl.pallas_call(functools.partial(layer_kernel, n, q), out_shape=jax.Shape...  138 us

profile of v3, /device:TPU:0, one launch (start us, length us, event | category | flops | bytes accessed | tf_op | source)
XLA Modules:
  0.0 140.3 jit_solution(7590024298631893167)
XLA Ops:
  0.0 138.1 %shard_map.64 = bf16[256,1792]{1,0:T(8,128)(2,1)} custom-call(bf16[256,1792]{1,0:T(8,128)(2,1)} %tok.1, s32[8,256]{1,0:T(8,128)} %bitcast.6, f32[8,256]{1,0:T(8,128)} %bitcast.7, s32[8]{0:T(128)} %owner.1, bf16[1792,2,1024]{2,1,0:T(2,128)(2,1)} %bitcast.4, bf16[1024,1792]{1,0:T(8,128)(2,1)} %bitcast.5), custom_call_target="tpu_custom_call" | custom-call | tf_op jit(solution)/shard_map/pallas_call | solution.py:379
  138.1 2.2 %copy.8 = bf16[256,1792]{1,0:T(8,128)(2,1)} copy(bf16[256,1792]{1,0:T(8,128)(2,1)} %shard_map.64) | data formatting | bytes 1835008

commit v4 on v2

--- a/solution.py
+++ b/solution.py
@@ -78,8 +78,12 @@
         hot = (code[pl.ds(partner(me, k, n), 1), :] == slot_iota).astype(F32).astype(BF16)
         return jnp.dot(hot, tok[...], preferred_element_type=F32).astype(BF16)
 
+    def turn(i):
+        half = n // 2
+        return (i % 2) * (n - (i + 1) // 2) + (1 - i % 2) * ((half - i // 2) % half)
+
     def dispatch(i, c):
-        k = n - i
+        k = turn(i)
         send[k] = pick(k)
         a_copy(k).start()
         return c
@@ -158,15 +162,15 @@
     def stage(i, c):
         @pl.when(i < n)
         def _():
-            project((n - i) % n)
+            project(turn(i))
+
+        @pl.when(i >= 2)
+        def _():
+            finish(turn(i - 2))
 
         @pl.when((i >= 1) & (i <= n))
         def _():
-            activate((n - i + 1) % n)
-
-        @pl.when(i >= 2)
-        def _():
-            finish((n - i + 2) % n)
+            activate(turn(i - 1))
 
         return c
 

time: 138 us -> 138 us (level)
  no operation moved by 1% of the time
where the time goes in v4:
time: 138 us; the launch traced here: 137 us
  Pallas kernels  135 us (98%)
  local copies, waits for them, and re-layouts  2.16 us (2%)
    pallas_call x1, Pallas kernels, on_device(): pl.pallas_call(functools.partial(layer_kernel, n, q), out_shape=jax.Shape...  135 us

profile of v4, /device:TPU:0, one launch (start us, length us, event | category | flops | bytes accessed | tf_op | source)
XLA Modules:
  0.0 137.3 jit_solution(8583813274424510955)
XLA Ops:
  0.0 135.2 %shard_map.64 = bf16[256,1792]{1,0:T(8,128)(2,1)} custom-call(bf16[256,1792]{1,0:T(8,128)(2,1)} %tok.1, s32[8,256]{1,0:T(8,128)} %bitcast.6, f32[8,256]{1,0:T(8,128)} %bitcast.7, s32[8]{0:T(128)} %owner.1, bf16[1792,2,1024]{2,1,0:T(2,128)(2,1)} %bitcast.4, bf16[1024,1792]{1,0:T(8,128)(2,1)} %bitcast.5), custom_call_target="tpu_custom_call" | custom-call | tf_op jit(solution)/shard_map/pallas_call | solution.py:275
  135.2 2.2 %copy.8 = bf16[256,1792]{1,0:T(8,128)(2,1)} copy(bf16[256,1792]{1,0:T(8,128)(2,1)} %shard_map.64) | data formatting | bytes 1835008
